TPU v7x, 32 devices: a whole 2x2x4 slice. The times are simulated.
32 devices in a mesh: grid: 8 (over z, x), chan: 4 (over y, core).
Axes of the slice: x: 2, y: 2, z: 4, core: 2. Of those that a mesh axis runs over, the one named last changes fastest.
Arguments:
- volt: float32 [2, 128, 4096, 512], P(None, None, 'grid', 'chan'), may hold values from -13 to 13
- placement: int32 [4096], P('grid'), may hold values from 0 to 63, as said below
- flags: int32 [4096], P('grid'), may hold values 0 or 1
Outputs:
- sky_image: float32 [64, 64], P('chan', 'grid')
Inputs may be any that keep to these rules, and one draw needn't show every extreme that they name: `placement`: within every grid row r, antennas r * 64 to (r + 1) * 64 - 1 take each column 0 to 63 exactly once.
All inputs are finite; a program needn't handle non-finite values. No bound on the sum of `flags` on one device may be relied on, other than what follows from the above.
Results may differ from a plain program's by a relative error of at most 0.0001.
Values sent between devices are 32-bit elements; how exact they have to be, the bound alone decides.
No kernel may reach another device: no remote copies, remote signals or barrier semaphores. Data moves between devices by JAX's collectives and lax.ppermute only.
A program may use at most 320 MiB of HBM per device.

v0:
```python
import math

import jax
import jax.numpy as jnp
from jax import lax
from jax.sharding import PartitionSpec as P

NROW = 64
GRID_COLUMNS = 64
CHANNELS = 512
TIMES = 128


def fourier_tables(length, left, right):
    phase_ids = left * right % length
    turned = phase_ids.astype(jnp.float32) * (2.0 * math.pi / length)
    return (jnp.cos(turned), jnp.sin(turned))


def row_tables():
    row_ids = lax.broadcasted_iota(jnp.int32, (NROW, NROW), 0)
    frequency_index = lax.broadcasted_iota(jnp.int32, (NROW, NROW), 1)
    return fourier_tables(NROW, row_ids, frequency_index)


def column_power(pieces):
    piece_re, piece_im = pieces
    x_cos, x_sin = row_tables()
    col_re = jnp.einsum(
        "txvc,xu->tuvc", piece_re, x_cos, precision=lax.Precision.HIGHEST
    ) + jnp.einsum("txvc,xu->tuvc", piece_im, x_sin, precision=lax.Precision.HIGHEST)
    col_im = jnp.einsum(
        "txvc,xu->tuvc", piece_im, x_cos, precision=lax.Precision.HIGHEST
    ) - jnp.einsum("txvc,xu->tuvc", piece_re, x_sin, precision=lax.Precision.HIGHEST)
    return jnp.sum(col_re * col_re + col_im * col_im, axis=3)


def on_device(volt, placement, flags):
    samples = volt.shape[1]
    local_antenna_count = volt.shape[2]
    chan_here = volt.shape[3]
    local_row_count = local_antenna_count // GRID_COLUMNS
    frequency_index = lax.broadcasted_iota(jnp.int32, (1, GRID_COLUMNS), 1)
    row_cosine, row_sine = fourier_tables(
        GRID_COLUMNS, placement.reshape(local_antenna_count, 1), frequency_index
    )
    active_mask = flags.astype(jnp.float32).reshape(local_antenna_count, 1)
    row_cosine = (active_mask * row_cosine).reshape(local_row_count, GRID_COLUMNS, GRID_COLUMNS)
    row_sine = (active_mask * row_sine).reshape(local_row_count, GRID_COLUMNS, GRID_COLUMNS)
    volt_re = volt[0].reshape(samples, local_row_count, GRID_COLUMNS, chan_here)
    volt_im = volt[1].reshape(samples, local_row_count, GRID_COLUMNS, chan_here)
    first_re = jnp.einsum(
        "txac,xav->txvc", volt_re, row_cosine, precision=lax.Precision.HIGHEST
    ) + jnp.einsum("txac,xav->txvc", volt_im, row_sine, precision=lax.Precision.HIGHEST)
    first_im = jnp.einsum(
        "txac,xav->txvc", volt_im, row_cosine, precision=lax.Precision.HIGHEST
    ) - jnp.einsum("txac,xav->txvc", volt_re, row_sine, precision=lax.Precision.HIGHEST)
    power_map = column_power(
        (
            lax.all_to_all(first_re, "grid", split_axis=2, concat_axis=1, tiled=True),
            lax.all_to_all(first_im, "grid", split_axis=2, concat_axis=1, tiled=True),
        )
    )
    image_part = jnp.sum(power_map, axis=0)
    summed = lax.psum_scatter(image_part, "chan", scatter_dimension=0, tiled=True)
    return summed * (1.0 / (TIMES * CHANNELS * NROW * GRID_COLUMNS))


def solution(mesh):
    return jax.shard_map(
        on_device,
        mesh=mesh,
        in_specs=(P(None, None, "grid", "chan"), P("grid"), P("grid")),
        out_specs=P("chan", "grid"),
        check_vma=False,
    )
```

profile of v0, /device:TPU:0, one launch (start us, length us, event | category | flops | bytes accessed | tf_op | source)
XLA Modules:
  0.0 1769.1 jit_solution(17588907960047816128)
XLA Ops:
  6.5 0.7 convert_element_type.18
  7.2 0.1 mul.81
  7.3 0.8 mul.83
  8.1 42.7 %fusion.92 = (f32[1,128,512,128]{3,2,1,0:T(8,128)}, f32[1,128,512,128]{3,2,1,0:T(8,128)}) fusion(f32[2,128,512,128]{3,2,1,0:T(8,128)} %param.3), kind=kLoop, calls=%fused_computation.90 | loop fusion | bytes 134217728 | tf_op jit(solution)/shard_map/slice | solution.py:50
  50.8 37.3 %fusion.14 = f32[8,64,128,128]{3,1,2,0:T(8,128)} fusion(f32[128,8,64,128]{3,2,1,0:T(8,128)} %bitcast.58, s32[8,64]{1,0:T(8,128)S(1)} %mul.83, f32[8,64]{1,0:T(8,128)S(1)} %mul.81), kind=kOutput, calls=%fused_computation.17 | convolution fusion | flops 6442942464 | bytes 67112960 | tf_op jit(solution)/shard_map/txac,xav->txvc/dot_general | solution.py:54
  88.0 41.5 %add_bitcast_fusion = f32[128,8,64,128]{3,2,0,1:T(8,128)} fusion(f32[8,64,128,128]{3,1,2,0:T(8,128)} %fusion.14, f32[128,8,64,128]{3,2,1,0:T(8,128)} %bitcast.56, s32[8,64]{1,0:T(8,128)S(1)} %mul.83, f32[8,64]{1,0:T(8,128)S(1)} %mul.81), kind=kOutput, calls=%fused_computation.10 | convolution fusion | flops 6451331072 | bytes 100667392 | tf_op jit(solution)/shard_map/txac,xav->txvc/dot_general | solution.py:52
  129.5 27.5 %copy.14 = f32[128,8,64,128]{3,0,1,2:T(8,128)} copy(f32[128,8,64,128]{3,2,0,1:T(8,128)} %add_bitcast_fusion) | data formatting | bytes 67108864 | tf_op jit(solution)/shard_map/add | solution.py:52
  157.1 7.9 all-to-all-start
  164.9 37.3 %fusion.12 = f32[8,64,128,128]{3,1,2,0:T(8,128)} fusion(f32[128,8,64,128]{3,2,1,0:T(8,128)} %bitcast.59, s32[8,64]{1,0:T(8,128)S(1)} %mul.83, f32[8,64]{1,0:T(8,128)S(1)} %mul.81), kind=kOutput, calls=%fused_computation.15 | convolution fusion | flops 6442942464 | bytes 67112960 | tf_op jit(solution)/shard_map/txac,xav->txvc/dot_general | solution.py:55
  202.2 41.4 %subtract_bitcast_fusion = f32[128,8,64,128]{3,2,0,1:T(8,128)} fusion(f32[8,64,128,128]{3,1,2,0:T(8,128)} %fusion.12, f32[128,8,64,128]{3,2,1,0:T(8,128)} %bitcast.57, s32[8,64]{1,0:T(8,128)S(1)} %mul.83, f32[8,64]{1,0:T(8,128)S(1)} %mul.81), kind=kOutput, calls=%fused_computation.9 | convolution fusion | flops 6451331072 | bytes 100667392 | tf_op jit(solution)/shard_map/txac,xav->txvc/dot_general | solution.py:57
  243.6 27.5 %copy.18 = f32[128,8,64,128]{3,0,1,2:T(8,128)} copy(f32[128,8,64,128]{3,2,0,1:T(8,128)} %subtract_bitcast_fusion) | data formatting | bytes 67108864 | tf_op jit(solution)/shard_map/sub | solution.py:55
  271.1 617.9 %all-to-all-done = f32[128,8,64,128]{3,0,1,2:T(8,128)} async-done(((f32[128,8,64,128]{3,0,1,2:T(8,128)}), f32[128,8,64,128]{3,0,1,2:T(8,128)}, u32[]{:S(2)}, u32[]{:S(2)}) %all-to-all-start) | async-done | bytes 33554464 | tf_op jit(solution)/shard_map/all_to_all | solution.py:60
  889.0 7.1 all-to-all-start.1
  896.1 0.0 reduce-scatter.4.cloned.1.call-start
  896.2 66.7 %fusion = f32[64,128,8,128]{3,0,2,1:T(8,128)} fusion(f32[128,8,8,8,128]{4,0,1,3,2:T(8,128)} %bitcast.9), kind=kOutput, calls=%fused_computation | convolution fusion | flops 6442508288 | bytes 67108864 | tf_op jit(solution)/shard_map/txvc,xu->tuvc/dot_general | solution.py:34
  962.9 66.7 %fusion.2 = f32[64,128,8,128]{3,0,2,1:T(8,128)} fusion(f32[128,8,8,8,128]{4,0,1,3,2:T(8,128)} %bitcast.9), kind=kOutput, calls=%fused_computation.2 | convolution fusion | flops 6442508288 | bytes 67108864 | tf_op jit(solution)/shard_map/txvc,xu->tuvc/dot_general | solution.py:29
  1029.5 588.6 %all-to-all-done.1 = f32[128,8,64,128]{3,0,1,2:T(8,128)} async-done(((f32[128,8,64,128]{3,0,1,2:T(8,128)}), f32[128,8,64,128]{3,0,1,2:T(8,128)}, u32[]{:S(2)}, u32[]{:S(2)}) %all-to-all-start.1) | async-done | bytes 33554464 | tf_op jit(solution)/shard_map/all_to_all | solution.py:61
  1618.2 66.4 %fusion.4 = f32[64,128,8,128]{3,0,2,1:T(8,128)} fusion(f32[128,8,8,8,128]{4,0,1,3,2:T(8,128)} %bitcast.17), kind=kOutput, calls=%fused_computation.4 | convolution fusion | flops 6442508288 | bytes 67108864 | tf_op jit(solution)/shard_map/txvc,xu->tuvc/dot_general | solution.py:32
  1684.6 57.1 %add_reduce_fusion = f32[64,8]{0,1:T(8,128)S(1)} fusion(f32[64,128,8,128]{3,0,2,1:T(8,128)} %fusion.4, f32[64,128,8,128]{3,0,2,1:T(8,128)} %fusion, f32[64,128,8,128]{3,0,2,1:T(8,128)} %fusion.2, f32[128,8,8,8,128]{4,0,1,3,2:T(8,128)} %bitcast.17), kind=kOutput, calls=%fused_computation.8 | convolution fusion | flops 6492839424 | bytes 134219776 | tf_op jit(solution)/shard_map/txvc,xu->tuvc/dot_general | solution.py:31
  1741.7 0.7 copy.24
  1742.4 0.0 reduce-scatter.4.cloned.1.call-update
  1742.4 18.3 %reduce-scatter.4.cloned.1.call-done = f32[16,8]{1,0:T(8,128)} async-done(((f32[64,8]{1,0:T(8,128)}), f32[16,8]{1,0:T(8,128)}) %reduce-scatter.4.cloned.1.call-update) | async-done | bytes 528
  1760.7 0.8 copy.25
  1761.5 0.6 broadcast_multiply_fusion
Async XLA Ops:
  157.1 731.9 %all-to-all-start = ((f32[128,8,64,128]{3,0,1,2:T(8,128)}), f32[128,8,64,128]{3,0,1,2:T(8,128)}, u32[]{:S(2)}, u32[]{:S(2)}) async-start(f32[128,8,64,128]{3,0,1,2:T(8,128)} %copy.14), calls=%async_computation | async-start | bytes 67108864 | tf_op jit(solution)/shard_map/all_to_all | solution.py:60
  889.0 729.2 %all-to-all-start.1 = ((f32[128,8,64,128]{3,0,1,2:T(8,128)}), f32[128,8,64,128]{3,0,1,2:T(8,128)}, u32[]{:S(2)}, u32[]{:S(2)}) async-start(f32[128,8,64,128]{3,0,1,2:T(8,128)} %copy.18), calls=%async_computation.1 | async-start | bytes 67108864 | tf_op jit(solution)/shard_map/all_to_all | solution.py:61
  896.1 864.6 %reduce-scatter.4.cloned.1.call-start = ((), (), s32[]{:S(2)}) async-start(), calls=%async_computation.3 | async-start | bytes 40960
Sparse Core Ops, SparseCore 0:
  1742.6 18.1 reduce-scatter.3
where the time goes:
time: 1780 us; the launch traced here: 1770 us
  waiting for transfers between devices  1220 us (69%)
  matrix products  414 us (23%)
  local copies, waits for them, and re-layouts  100 us (6%)
    all_to_all x1, waiting for transfers between devices, on_device(): lax.all_to_all(first_re, 'grid', split_axis=2, concat_axis=1, tiled=True)  618 us
    all_to_all x1, waiting for transfers between devices, on_device(): lax.all_to_all(first_im, 'grid', split_axis=2, concat_axis=1, tiled=True)  589 us
    dot_general x1, matrix products, column_power(): jnp.einsum('txvc,xu->tuvc', piece_re, x_sin, precision=lax.Precision.HIGH...  66.7 us
    dot_general x1, matrix products, column_power(): jnp.einsum('txvc,xu->tuvc', piece_re, x_cos, precision=lax.Precision.HIGH...  66.7 us
    dot_general x1, matrix products, column_power(): jnp.einsum('txvc,xu->tuvc', piece_im, x_cos, precision=lax.Precision.HIGH...  66.4 us
    dot_general x1, matrix products, column_power(): jnp.einsum('txvc,xu->tuvc', piece_im, x_sin, precision=lax.Precision.HIGH...  57.1 us
    slice x1, local copies, waits for them, and re-layouts, on_device(): volt_re = volt[0].reshape(samples, local_row_count, GRID_COLUMNS, chan_here)  42.7 us
    dot_general x1, matrix products, on_device(): jnp.einsum('txac,xav->txvc', volt_re, row_cosine, precision=lax.Precision...  41.5 us
  transfers between devices with their start and end apart: 3, of which 3 were waited for; matrix products, arithmetic and copies ran while one was open for 14% of the time, Pallas kernels for 0%

commit v1 on v0

v1 whole, which is shorter than its diff:
```python
import functools
import math

import jax
import jax.numpy as jnp
from jax import lax
from jax.experimental import pallas as pl
from jax.experimental.pallas import tpu as pltpu
from jax.sharding import PartitionSpec as P

NROW = 64
GRID_COLUMNS = 64
CHANNELS = 512
TIMES = 128
SUB = 8
QUANTUM = 32


def cosine(phase, length):
    turned = (phase % length).astype(jnp.float32) * (2.0 * math.pi / length)
    return jnp.cos(turned)


def halves(value):
    high = value.astype(jnp.bfloat16)
    low = (value - high.astype(jnp.float32)).astype(jnp.bfloat16)
    return high, low


def constant_halves(value):
    high = lax.reduce_precision(value, exponent_bits=8, mantissa_bits=7)
    return high.astype(jnp.bfloat16), (value - high).astype(jnp.bfloat16)


def mm(left, right):
    return jnp.dot(left, right, preferred_element_type=jnp.float32)


def pack_kernel(slots, first_ref, where_ref, volt_ref, out_ref):
    del first_ref
    ants = where_ref.shape[1]
    chans = volt_ref.shape[3]
    slot_ids = lax.broadcasted_iota(jnp.int32, (slots, ants), 0)
    pick = (slot_ids == where_ref[...]).astype(jnp.float32).astype(jnp.bfloat16)
    both = jnp.concatenate([volt_ref[0, 0], volt_ref[1, 0]], axis=1)
    high, low = halves(both)
    kept = mm(pick, high) + mm(pick, low)
    out_ref[0, 0, 0] = kept[:, :chans]
    out_ref[0, 0, 1] = kept[:, chans:]


def pack(volt, where, slots, group, first, count):
    _, samples, ants, chans = volt.shape
    per_dest = samples // group
    return pl.pallas_call(
        functools.partial(pack_kernel, slots),
        grid_spec=pltpu.PrefetchScalarGridSpec(
            num_scalar_prefetch=1,
            grid=(group, count),
            in_specs=[
                pl.BlockSpec((1, ants), lambda g, j, first: (0, 0)),
                pl.BlockSpec((2, 1, ants, chans), lambda g, j, first: (0, g * per_dest + first[0] + j, 0, 0)),
            ],
            out_specs=pl.BlockSpec((1, 1, 2, slots, chans), lambda g, j, first: (g, j, 0, 0, 0)),
        ),
        out_shape=jax.ShapeDtypeStruct((group, count, 2, slots, chans), jnp.float32),
        cost_estimate=pl.CostEstimate(
            flops=group * count * slots * ants * chans * 8,
            bytes_accessed=group * count * 8 * chans * (ants + slots),
            transcendentals=0,
        ),
        name="pack",
    )(jnp.full((1,), first, jnp.int32), where, volt)


def table_kernel(wave_high_ref, wave_low_ref, row_ref, term_ref, high_ref, low_ref):
    lines, terms = wave_high_ref.shape
    depth = row_ref.shape[2]
    rows = high_ref.shape[1] // lines
    hit = term_ref[0] == lax.broadcasted_iota(jnp.int32, (terms, depth), 0)
    hit = hit.astype(jnp.float32).astype(jnp.bfloat16)
    mine = row_ref[0] == lax.broadcasted_iota(jnp.int32, (rows, depth), 0)
    for wave_ref, out_ref in ((wave_high_ref, high_ref), (wave_low_ref, low_ref)):
        wave = mm(wave_ref[...], hit)
        spread = jnp.where(mine[None], wave[:, None, :], 0.0)
        out_ref[0] = spread.reshape(lines * rows, depth).astype(jnp.bfloat16)


def tables(wave_high, wave_low, row, term, rows):
    lines = wave_high.shape[0]
    groups, _, depth = row.shape
    out = jax.ShapeDtypeStruct((groups, lines * rows, depth), jnp.bfloat16)
    spec = pl.BlockSpec((1, lines * rows, depth), lambda d: (d, 0, 0))
    slot_spec = pl.BlockSpec((1, 1, depth), lambda d: (d, 0, 0))
    wave_spec = pl.BlockSpec(wave_high.shape, lambda d: (0, 0))
    return pl.pallas_call(
        table_kernel,
        grid=(groups,),
        in_specs=[wave_spec, wave_spec, slot_spec, slot_spec],
        out_specs=(spec, spec),
        out_shape=(out, out),
        cost_estimate=pl.CostEstimate(
            flops=groups * lines * rows * depth * 4,
            bytes_accessed=groups * lines * rows * depth * 4,
            transcendentals=0,
        ),
        name="tables",
    )(wave_high, wave_low, row, term)


def image_kernel(rows, got_ref, high_ref, low_ref, col_ref, acc_in_ref, acc_ref, mid_ref):
    step = pl.program_id(1)
    count = got_ref.shape[1]
    chans = got_ref.shape[4]
    depth = high_ref.shape[2]
    lines = high_ref.shape[1] // rows
    sides = [got_ref[:, j].reshape(depth, chans) for j in range(count)]
    data = jnp.concatenate(sides, axis=1) if count > 1 else sides[0]
    high, low = halves(data)
    some = 32

    def part(i, carry):
        span = pl.ds(pl.multiple_of(i * some * rows, some * rows), some * rows)
        coarse = high_ref[0, span, :]
        fine = low_ref[0, span, :]
        found = mm(coarse, high) + mm(coarse, low) + mm(fine, high)
        mid_ref[pl.ds(i * some, some), pl.ds(pl.multiple_of(step * rows, rows), rows), :] = found.reshape(
            some, rows, count * chans
        )
        return carry

    lax.fori_loop(0, lines // some, part, 0)

    @pl.when((step == 0) & (pl.program_id(0) == 0))
    def _():
        acc_ref[...] = acc_in_ref[...]

    @pl.when(step == pl.num_programs(1) - 1)
    def _():
        half = col_ref.shape[0] // 2

        def column(v, carry):
            line = mid_ref[pl.ds(2 * v, 2)].reshape(2 * mid_ref.shape[1], count * chans)
            line_high, line_low = halves(line)
            seen = mm(col_ref[...], jnp.concatenate([line_high, line_low, line_high], axis=0))
            seen = seen * seen
            power = seen[:half] + seen[half:]
            total = power[:, :chans]
            for j in range(1, count):
                total = total + power[:, j * chans : (j + 1) * chans]
            acc_ref[v] += total
            return carry

        lax.fori_loop(0, lines // 2, column, 0, unroll=4)


def image(got, high, low, col, acc, rows):
    sources, count, _, slots, chans = got.shape
    groups, tall, depth = high.shape
    each = sources // groups
    lines = tall // rows
    block = 2 if count % 2 == 0 else 1
    whole_acc = pl.BlockSpec(acc.shape, lambda p, d: (0, 0, 0))
    table_spec = pl.BlockSpec((1, tall, depth), lambda p, d: (d, 0, 0))
    return pl.pallas_call(
        functools.partial(image_kernel, rows),
        grid=(count // block, groups),
        in_specs=[
            pl.BlockSpec((each, block, 2, slots, chans), lambda p, d: (d, p, 0, 0, 0)),
            table_spec,
            table_spec,
            pl.BlockSpec(col.shape, lambda p, d: (0, 0)),
            whole_acc,
        ],
        out_specs=whole_acc,
        out_shape=jax.ShapeDtypeStruct(acc.shape, jnp.float32),
        scratch_shapes=[pltpu.VMEM((lines, groups * rows, block * chans), jnp.float32)],
        cost_estimate=pl.CostEstimate(
            flops=6 * groups * tall * depth * count * chans,
            bytes_accessed=4 * got.size + 4 * high.size + 8 * acc.size,
            transcendentals=0,
        ),
        name="image",
    )(got, high, low, col, acc)


def chunk_sizes(samples):
    if samples < 8 or samples % 8:
        return [samples]
    piece = samples // 8
    return [piece, 3 * piece, 3 * piece, piece]


def share(value, axes, size):
    return lax.all_to_all(jnp.broadcast_to(value[None], (size,) + value.shape), axes, 0, 0, tiled=True)


def on_device(group, others, volt, placement, flags):
    _, samples, ants, chans = volt.shape
    local_rows = ants // GRID_COLUMNS
    per_dest = samples // group
    each = max(1, SUB // local_rows)
    groups = group // each
    rows = local_rows * each

    codes = share(placement * 2 + flags, "grid", group)
    used = codes % 2
    upto = lax.broadcasted_iota(jnp.int32, (ants, ants), 0) <= lax.broadcasted_iota(jnp.int32, (ants, ants), 1)
    place = jnp.dot(
        used.astype(jnp.bfloat16), upto.astype(jnp.bfloat16), preferred_element_type=jnp.float32
    ).astype(jnp.int32)
    most = jnp.max(place[:, -1])
    where = jnp.where(used == 1, place - 1, -1)
    mine = lax.dynamic_slice_in_dim(where, lax.axis_index("grid"), 1, axis=0)
    cell = codes // 2 + lax.broadcasted_iota(jnp.int32, (group, ants), 1) // GRID_COLUMNS * GRID_COLUMNS + 1

    quarter = NROW // 4
    shape = (2 * NROW, 2 * NROW)
    line_ids = lax.broadcasted_iota(jnp.int32, shape, 0)
    term_ids = lax.broadcasted_iota(jnp.int32, shape, 1)
    turn = quarter * (term_ids // NROW)
    col_high, col_low = constant_halves(
        cosine((line_ids % NROW) * (term_ids % NROW) + quarter * (line_ids // NROW) - turn, NROW)
    )
    col = jnp.concatenate([col_high, col_high, col_low], axis=1)
    wave_high, wave_low = constant_halves(
        cosine((line_ids // 2) * (term_ids % NROW) + quarter * (line_ids % 2) - turn, NROW)
    )

    def with_slots(slots):
        def run(volt, where, mine, cell, col, wave_high, wave_low):
            hit = where[:, None, :] == lax.broadcasted_iota(jnp.int32, (1, slots, 1), 1)
            tag = jnp.sum(jnp.where(hit, cell[:, None, :], 0), axis=2) - 1
            slot_row = jnp.where(tag >= 0, tag // GRID_COLUMNS, -rows)
            slot_row = slot_row + lax.broadcasted_iota(jnp.int32, (group, slots), 0) % each * local_rows
            slot_col = tag % GRID_COLUMNS
            depth = each * 2 * slots
            twice = lambda a, b: jnp.stack([a, b], axis=1).reshape(groups, 1, depth)
            high, low = tables(
                wave_high,
                wave_low,
                twice(slot_row, slot_row),
                twice(slot_col, slot_col + GRID_COLUMNS),
                rows,
            )
            chunks = chunk_sizes(per_dest)
            acc = jnp.zeros((GRID_COLUMNS, NROW, chans), jnp.float32)
            packed = pack(volt, mine, slots, group, 0, chunks[0])
            first = chunks[0]
            behind = None
            for i in range(len(chunks)):
                got = lax.all_to_all(packed, "grid", split_axis=0, concat_axis=0, tiled=True)
                if behind is not None:
                    acc = image(behind, high, low, col, acc, rows)
                if i + 1 < len(chunks):
                    mine, acc = lax.optimization_barrier((mine, acc))
                    packed = pack(volt, mine, slots, group, first, chunks[i + 1])
                    first += chunks[i + 1]
                behind = got
            acc = image(behind, high, low, col, acc, rows)
            return jnp.sum(acc, axis=2)

        return run

    quantum = min(QUANTUM, ants)
    sizes = BUCKETS if BUCKETS else list(range(quantum, ants + 1, quantum))
    which = jnp.clip((most + quantum - 1) // quantum - 1, 0, len(sizes) - 1)
    power = lax.switch(
        which, [with_slots(s) for s in sizes], volt, where, mine, cell, col, wave_high, wave_low
    )
    blocks = power.T.reshape(others, NROW // others, group, GRID_COLUMNS // group)
    blocks = blocks.transpose(2, 0, 1, 3).reshape(group * others, -1)
    parts = lax.all_to_all(blocks, ("grid", "chan"), split_axis=0, concat_axis=0, tiled=True)
    summed = jnp.sum(parts, axis=0).reshape(NROW // others, GRID_COLUMNS // group)
    return summed * (1.0 / (TIMES * CHANNELS * NROW * GRID_COLUMNS))


BUCKETS = None


def solution(mesh):
    return jax.shard_map(
        functools.partial(on_device, mesh.shape["grid"], mesh.shape["chan"]),
        mesh=mesh,
        in_specs=(P(None, None, "grid", "chan"), P("grid"), P("grid")),
        out_specs=P("chan", "grid"),
        check_vma=False,
    )
```

time: 1780 us -> 1320 us (0.74)
  matrix products: 414 us -> 0.18 us
  Pallas kernels: 0 us -> 336 us
  waiting for transfers between devices: 1220 us -> 887 us
  local copies, waits for them, and re-layouts: 100 us -> 4.82 us
  loops' own time: 0 us -> 36.9 us
    dot_general x8 -> x1, matrix products: 414 us -> 0.18 us  [on_device(): jnp.dot(used.astype(jnp.bfloat16), upto.astype(jnp.bfloat16), preferred_e...]
    pallas_call x0 -> x9, Pallas kernels: none -> 336 us  [the longest x4 215 us: image(): pl.pallas_call(functools.partial(image_kernel, rows), grid=(count // bloc...]
    all_to_all x2 -> x5, waiting for transfers between devices: 1210 us -> 887 us  [the longest x4 881 us: run(): lax.all_to_all(packed, 'grid', split_axis=0, concat_axis=0, tiled=True)]
    slice x1 -> x0, local copies, waits for them, and re-layouts: 42.7 us -> none  [on_device(): volt_re = volt[0].reshape(samples, local_row_count, GRID_COLUMNS, chan_here)]
    another operation x0 -> x1, loops' own time: none -> 36.9 us  [on_device(): lax.switch(which, [with_slots(s) for s in sizes], volt, where, mine, cell...]
    add x1 -> x0, local copies, waits for them, and re-layouts: 27.5 us -> none  [on_device(): jnp.einsum('txac,xav->txvc', volt_re, row_cosine, precision=lax.Precision...]
    sub x1 -> x0, local copies, waits for them, and re-layouts: 27.5 us -> none  [on_device(): jnp.einsum('txac,xav->txvc', volt_im, row_cosine, precision=lax.Precision...]
    unnamed x2 -> x0, waiting for transfers between devices: 18.3 us -> none
  transfers between devices with their start and end apart: 3 -> 5, of which waited for: 3 -> 5; matrix products, arithmetic and copies ran while one was open for 14% -> 0% of each run, Pallas kernels for 0% -> 22%
where the time goes in v1:
time: 1320 us; the launch traced here: 1310 us
  waiting for transfers between devices  887 us (67%)
  Pallas kernels  336 us (25%)
  loops' own time  36.9 us (3%)
  starting transfers between devices  29.1 us (2%)
    all_to_all x4, waiting for transfers between devices, run(): lax.all_to_all(packed, 'grid', split_axis=0, concat_axis=0, tiled=True)  881 us
    pallas_call x4, Pallas kernels, image(): pl.pallas_call(functools.partial(image_kernel, rows), grid=(count // bloc...  215 us
    pallas_call x4, Pallas kernels, pack(): pl.pallas_call(functools.partial(pack_kernel, slots), grid_spec=pltpu.Pre...  110 us
    another operation x1, loops' own time, on_device(): lax.switch(which, [with_slots(s) for s in sizes], volt, where, mine, cell...  36.9 us
  transfers between devices with their start and end apart: 5, of which 5 were waited for; matrix products, arithmetic and copies ran while one was open for 0% of the time, Pallas kernels for 22%

profile of v1, /device:TPU:0, one launch (start us, length us, event | category | flops | bytes accessed | tf_op | source)
XLA Modules:
  0.0 1311.7 jit_solution(9003935388083486075)
XLA Ops:
  0.0 0.7 multiply_add_fusion
  0.7 0.6 broadcast_in_dim.295
  1.3 7.3 all-to-all-start.64
  8.7 0.6 reduce-precision_convert_fusion
  9.3 5.8 all-to-all-done.64
  15.2 0.2 fusion.79
  15.4 0.7 slice_reduce_fusion
  16.8 1280.1 %conditional.1 = (f32[64,64,128]{2,1,0:T(8,128)}, f32[]{:T(128)}, f32[]{:T(128)}) conditional(s32[]{:T(128)} %clamp.3, (s32[1,512]{1,0:T(1,128)S(1)}, f32[2,128,512,128]{3,2,1,0:T(8,128)}, s32[8,512]{1,0:T(8,128)S(1)}, s32[8,512]{1,0:T(8,128)S(1)}, bf16[128,128]{1,0:T(8,128)(2,1)S(1)}, ...), branch_computations={%region_1.3_spmd, %region_3.5_spmd, %region_5.7_spmd, %region_7.9_... | conditional | flops 137478897664 | bytes 589791360 | solution.py:268
  35.6 14.3 %pack.112 = f32[8,2,2,416,128]{4,3,2,1,0:T(8,128)} custom-call(s32[1]{0:T(128)} %constant.1025.clone.first_ref, s32[1,512]{1,0:T(1,128)S(1)} %get-tuple-element.426.where_ref, f32[2,128,512,128]{3,2,1,0:T(8,128)} %get-tuple-element.415.volt_ref), custom_call_target="tpu_custom_call" | custom-call | flops 3489660928 | bytes 15204352 | tf_op jit(solution)/shard_map/cond/branch_12_fun/pack/pallas_call | solution.py:55
  49.9 4.8 all-to-all-start.48
  54.8 1.5 broadcast.3465.acc_in_ref
  56.3 40.5 %pack.113 = f32[8,6,2,416,128]{4,3,2,1,0:T(8,128)} custom-call(s32[1]{0:T(128)} %constant.1033.clone.first_ref, s32[1,512]{1,0:T(1,128)S(1)} %get-tuple-element.426.where_ref, f32[2,128,512,128]{3,2,1,0:T(8,128)} %get-tuple-element.415.volt_ref), custom_call_target="tpu_custom_call" | custom-call | flops 10468982784 | bytes 45613056 | tf_op jit(solution)/shard_map/cond/branch_12_fun/pack/pallas_call | solution.py:55
  96.8 106.1 %all-to-all-done.48.got_ref = f32[8,2,2,416,128]{4,3,2,1,0:T(8,128)} async-done(((f32[8,2,2,416,128]{4,3,2,1,0:T(8,128)}), f32[8,2,2,416,128]{4,3,2,1,0:T(8,128)}, u32[]{:S(2)}, u32[]{:S(2)}) %all-to-all-start.48) | async-done | bytes 6815776 | tf_op jit(solution)/shard_map/cond/branch_12_fun/all_to_all | solution.py:252
  203.0 6.0 all-to-all-start.49
  209.0 0.8 select_reduce_fusion.12
  209.9 0.7 reshape.1767.row_ref
  210.7 0.7 reshape.1768.term_ref
  211.4 11.9 tables.28
  223.3 29.2 %image.112.acc_in_ref = f32[64,64,128]{2,1,0:T(8,128)} custom-call(f32[8,2,2,416,128]{4,3,2,1,0:T(8,128)} %all-to-all-done.48.got_ref, bf16[8,1024,832]{2,1,0:T(8,128)(2,1)} %get-tuple-element.420.high_ref, bf16[8,1024,832]{2,1,0:T(8,128)(2,1)} %get-tuple-element.421.low_ref, bf16[128,384]{1,0:T(8,128)(2,1)S(1)} %get-tuple-element.422.col_ref, ...), custom_call_target="tpu_custom_call" | custom-call | flops 10468982784 | bytes 38273024 | tf_op jit(solution)/shard_map/cond/branch_12_fun/image/pallas_call | solution.py:165
  252.5 40.5 %pack.115 = f32[8,6,2,416,128]{4,3,2,1,0:T(8,128)} custom-call(s32[1]{0:T(128)} %constant.1034.clone.first_ref, s32[1,512]{1,0:T(1,128)S(1)} %get-tuple-element.426.where_ref, f32[2,128,512,128]{3,2,1,0:T(8,128)} %get-tuple-element.415.volt_ref), custom_call_target="tpu_custom_call" | custom-call | flops 10468982784 | bytes 45613056 | tf_op jit(solution)/shard_map/cond/branch_12_fun/pack/pallas_call | solution.py:55
  293.0 355.5 %all-to-all-done.49.got_ref = f32[8,6,2,416,128]{4,3,2,1,0:T(8,128)} async-done(((f32[8,6,2,416,128]{4,3,2,1,0:T(8,128)}), f32[8,6,2,416,128]{4,3,2,1,0:T(8,128)}, u32[]{:S(2)}, u32[]{:S(2)}) %all-to-all-start.49) | async-done | bytes 20447264 | tf_op jit(solution)/shard_map/cond/branch_12_fun/all_to_all | solution.py:252
  648.5 6.0 all-to-all-start.51
  654.6 78.3 %image.113.acc_in_ref = f32[64,64,128]{2,1,0:T(8,128)} custom-call(f32[8,6,2,416,128]{4,3,2,1,0:T(8,128)} %all-to-all-done.49.got_ref, bf16[8,1024,832]{2,1,0:T(8,128)(2,1)} %get-tuple-element.420.high_ref, bf16[8,1024,832]{2,1,0:T(8,128)(2,1)} %get-tuple-element.421.low_ref, bf16[128,384]{1,0:T(8,128)(2,1)S(1)} %get-tuple-element.422.col_ref, ...), custom_call_target="tpu_custom_call" | custom-call | flops 31406948352 | bytes 51904512 | tf_op jit(solution)/shard_map/cond/branch_12_fun/image/pallas_call | solution.py:165
  732.9 14.3 %pack.114 = f32[8,2,2,416,128]{4,3,2,1,0:T(8,128)} custom-call(s32[1]{0:T(128)} %constant.1023.clone.first_ref, s32[1,512]{1,0:T(1,128)S(1)} %get-tuple-element.426.where_ref, f32[2,128,512,128]{3,2,1,0:T(8,128)} %get-tuple-element.415.volt_ref), custom_call_target="tpu_custom_call" | custom-call | flops 3489660928 | bytes 15204352 | tf_op jit(solution)/shard_map/cond/branch_12_fun/pack/pallas_call | solution.py:55
  747.1 347.8 %all-to-all-done.51.got_ref = f32[8,6,2,416,128]{4,3,2,1,0:T(8,128)} async-done(((f32[8,6,2,416,128]{4,3,2,1,0:T(8,128)}), f32[8,6,2,416,128]{4,3,2,1,0:T(8,128)}, u32[]{:S(2)}, u32[]{:S(2)}) %all-to-all-start.51) | async-done | bytes 20447264 | tf_op jit(solution)/shard_map/cond/branch_12_fun/all_to_all | solution.py:252
  1095.0 4.9 all-to-all-start.50
  1099.9 78.2 %image.114.acc_in_ref = f32[64,64,128]{2,1,0:T(8,128)} custom-call(f32[8,6,2,416,128]{4,3,2,1,0:T(8,128)} %all-to-all-done.51.got_ref, bf16[8,1024,832]{2,1,0:T(8,128)(2,1)} %get-tuple-element.420.high_ref, bf16[8,1024,832]{2,1,0:T(8,128)(2,1)} %get-tuple-element.421.low_ref, bf16[128,384]{1,0:T(8,128)(2,1)S(1)} %get-tuple-element.422.col_ref, ...), custom_call_target="tpu_custom_call" | custom-call | flops 31406948352 | bytes 51904512 | tf_op jit(solution)/shard_map/cond/branch_12_fun/image/pallas_call | solution.py:165
  1178.0 71.5 %all-to-all-done.50.got_ref = f32[8,2,2,416,128]{4,3,2,1,0:T(8,128)} async-done(((f32[8,2,2,416,128]{4,3,2,1,0:T(8,128)}), f32[8,2,2,416,128]{4,3,2,1,0:T(8,128)}, u32[]{:S(2)}, u32[]{:S(2)}) %all-to-all-start.50) | async-done | bytes 6815776 | tf_op jit(solution)/shard_map/cond/branch_12_fun/all_to_all | solution.py:252
  1249.5 29.3 %image.115 = f32[64,64,128]{2,1,0:T(8,128)} custom-call(f32[8,2,2,416,128]{4,3,2,1,0:T(8,128)} %all-to-all-done.50.got_ref, bf16[8,1024,832]{2,1,0:T(8,128)(2,1)} %get-tuple-element.420.high_ref, bf16[8,1024,832]{2,1,0:T(8,128)(2,1)} %get-tuple-element.421.low_ref, bf16[128,384]{1,0:T(8,128)(2,1)S(1)} %get-tuple-element.422.col_ref, ...), custom_call_target="tpu_custom_call" | custom-call | flops 10468982784 | bytes 38273024 | tf_op jit(solution)/shard_map/cond/branch_12_fun/image/pallas_call | solution.py:165
  1296.8 2.2 reduce_sum.182
  1299.5 10.7 all_to_all.274
  1310.3 0.7 copy.45
  (20 shorter events, 0.7 us)
Async XLA Ops:
  1.3 13.9 %all-to-all-start.64 = ((s32[8,1,512]{2,1,0:T(1,128)}), s32[8,1,512]{2,1,0:T(1,128)S(1)}, u32[]{:S(2)}, u32[]{:S(2)}) async-start(s32[8,1,512]{2,1,0:T(1,128)} %broadcast_in_dim.295), calls=%async_computation.64 | async-start | bytes 32768 | tf_op jit(solution)/shard_map/all_to_all | solution.py:195
  49.9 153.0 %all-to-all-start.48 = ((f32[8,2,2,416,128]{4,3,2,1,0:T(8,128)}), f32[8,2,2,416,128]{4,3,2,1,0:T(8,128)}, u32[]{:S(2)}, u32[]{:S(2)}) async-start(f32[8,2,2,416,128]{4,3,2,1,0:T(8,128)} %pack.112), calls=%async_computation.48 | async-start | bytes 13631488 | tf_op jit(solution)/shard_map/cond/branch_12_fun/all_to_all | solution.py:252
  203.0 445.6 %all-to-all-start.49 = ((f32[8,6,2,416,128]{4,3,2,1,0:T(8,128)}), f32[8,6,2,416,128]{4,3,2,1,0:T(8,128)}, u32[]{:S(2)}, u32[]{:S(2)}) async-start(f32[8,6,2,416,128]{4,3,2,1,0:T(8,128)} %pack.113), calls=%async_computation.49 | async-start | bytes 40894464 | tf_op jit(solution)/shard_map/cond/branch_12_fun/all_to_all | solution.py:252
  648.5 446.4 %all-to-all-start.51 = ((f32[8,6,2,416,128]{4,3,2,1,0:T(8,128)}), f32[8,6,2,416,128]{4,3,2,1,0:T(8,128)}, u32[]{:S(2)}, u32[]{:S(2)}) async-start(f32[8,6,2,416,128]{4,3,2,1,0:T(8,128)} %pack.115), calls=%async_computation.51 | async-start | bytes 40894464 | tf_op jit(solution)/shard_map/cond/branch_12_fun/all_to_all | solution.py:252
  1095.0 154.6 %all-to-all-start.50 = ((f32[8,2,2,416,128]{4,3,2,1,0:T(8,128)}), f32[8,2,2,416,128]{4,3,2,1,0:T(8,128)}, u32[]{:S(2)}, u32[]{:S(2)}) async-start(f32[8,2,2,416,128]{4,3,2,1,0:T(8,128)} %pack.114), calls=%async_computation.50 | async-start | bytes 13631488 | tf_op jit(solution)/shard_map/cond/branch_12_fun/all_to_all | solution.py:252
